TPU v7x, 32 devices: a whole 2x2x4 slice. The times are simulated.
32 devices in a mesh: row: 4 (over x, core), col: 8 (over z, y).
Axes of the slice: x: 2, y: 2, z: 4, core: 2. Of those that a mesh axis runs over, the one named last changes fastest.
Arguments:
- hidden: bfloat16 [128, 8192], P('col', 'row'), may hold values from -6 to 6
- w_gate: bfloat16 [8192, 16384], P('row', 'col'), may hold values from -0.0625 to 0.0625
- w_up: bfloat16 [8192, 16384], P('row', 'col'), may hold values from -0.0625 to 0.0625
- prior: float32 [16384, 16384], P('row', 'col'), may hold values from -1 to 12, as said below
- rhs: float32 [16384, 4096], P('row', 'col'), may hold values from -6 to 6
Outputs:
- factored: float32 [16384, 16384], P('row', 'col')
- right_out: float32 [16384, 4096], P('row', 'col')
Inputs may be any that keep to these rules, and one draw needn't show every extreme that they name: prior is symmetric and positive definite, with smallest eigenvalue 0.1 or more.
All inputs are finite; a program needn't handle non-finite values.
Results may differ from a plain program's by a relative error of at most 0.0003.
Values may be sent and summed in bfloat16 or wider, within the bound.
A program may use at most 192 MiB of HBM per device.

v0:
```python
import jax
import jax.numpy as jnp
from jax import lax
from jax.sharding import PartitionSpec as P

P_SIZE = 128
PANELS = 2
DAMP = 0.5


def from_root(value, axis, source):
    kept = jnp.where(lax.axis_index(axis) == source, value, 0).astype(value.dtype)
    return lax.psum(kept, axis)


def local(hidden, w_gate, w_up, prior, rhs):
    rows_count = lax.axis_size("row")
    cols_count = lax.axis_size("col")
    row_id = lax.axis_index("row")
    col_id = lax.axis_index("col")
    ratio = cols_count // rows_count
    height, width = prior.shape
    tokens = lax.all_gather(hidden, "col", axis=0, tiled=True)
    gate_part = jnp.dot(tokens, w_gate, preferred_element_type=jnp.float32)
    up_part = jnp.dot(tokens, w_up, preferred_element_type=jnp.float32)
    gate, upward = lax.psum((gate_part, up_part), "row")
    keys = jax.nn.silu(gate) * upward
    samples = keys.shape[0]
    regrouped = lax.all_to_all(keys, "col", split_axis=0, concat_axis=1, tiled=True)
    own_part = lax.dynamic_slice_in_dim(regrouped, row_id * height, height, 1)
    row_keys = lax.all_gather(own_part, "col", axis=0, tiled=True)
    row_global = row_id * height + lax.iota(jnp.int32, height)
    col_global = col_id * width + lax.iota(jnp.int32, width)
    outer = lax.dot_general(
        row_keys,
        keys,
        (((0,), (0,)), ((), ())),
        precision=lax.Precision.HIGHEST,
        preferred_element_type=jnp.float32,
    )
    work = prior + outer / samples
    work = work + jnp.where(row_global[:, None] == col_global[None, :], DAMP, 0.0).astype(
        jnp.float32
    )
    right = rhs
    offsets = lax.iota(jnp.int32, P_SIZE)
    for panel in range(PANELS):
        start = panel * P_SIZE
        stop = start + P_SIZE
        pivot = jnp.linalg.cholesky(work[start:stop, start:stop])
        pivot = from_root(pivot, "row", 0)
        column = work[:, start:stop]
        solved = jax.scipy.linalg.solve_triangular(pivot, column.T, lower=True).T
        placed = jnp.zeros_like(solved).at[start:stop].set(pivot)
        in_pivot = (row_global >= start) & (row_global < stop)
        beyond = row_global >= stop
        factor_cols = jnp.where(in_pivot[:, None], placed, jnp.where(beyond[:, None], solved, 0.0))
        factor_cols = from_root(factor_cols, "col", 0)
        matching = lax.dynamic_slice_in_dim(factor_cols, col_id % ratio * width, width, 0)
        across = from_root(matching, "row", col_id // ratio)
        lower_rows = jnp.where(beyond[:, None], factor_cols, 0.0)
        upper_cols = jnp.where((col_global >= stop)[:, None], across, 0.0)
        work = work - lax.dot_general(
            lower_rows,
            upper_cols,
            (((1,), (1,)), ((), ())),
            precision=lax.Precision.HIGHEST,
            preferred_element_type=jnp.float32,
        )
        solution = jax.scipy.linalg.solve_triangular(
            factor_cols[start:stop], right[start:stop], lower=True
        )
        solution = from_root(solution, "row", 0)
        right = right - jnp.dot(
            lower_rows,
            solution,
            precision=lax.Precision.HIGHEST,
            preferred_element_type=jnp.float32,
        )
        right = right.at[start:stop].set(jnp.where(row_id == 0, solution, right[start:stop]))
        keep_factor = (row_global[:, None] >= start + offsets[None, :]) & (col_id == 0)
        work = work.at[:, start:stop].set(jnp.where(keep_factor, factor_cols, work[:, start:stop]))
    return (work, right)


def solution(mesh):
    return jax.shard_map(
        local,
        mesh=mesh,
        in_specs=(
            P("col", "row"),
            P("row", "col"),
            P("row", "col"),
            P("row", "col"),
            P("row", "col"),
        ),
        out_specs=(P("row", "col"), P("row", "col")),
        check_vma=False,
    )
```

profile of v0, /device:TPU:0, one launch (start us, length us, event | category | flops | bytes accessed | tf_op | source)
XLA Modules:
  0.0 747.9 jit_solution(3485265117234313394)
XLA Ops:
  7.2 0.0 all-reduce.25.cloned.1.call-start
  7.2 33.4 %all_gather.6 = bf16[128,2048]{1,0:T(8,128)(2,1)S(1)} all-gather(bf16[16,2048]{1,0:T(8,128)(2,1)} %param.22), channel_id=1, replica_groups=mesh['row'=4,'col'=8] {'col'}, dimensions={0}, use_global_device_ids=true | all-gather | bytes 589824 | tf_op jit(solution)/shard_map/all_gather | solution.py:23
  40.6 5.8 fusion.52
  46.4 2.3 fusion.53
  48.7 0.0 all-reduce.25.cloned.1.call-update
  48.7 52.7 %all-reduce.25.cloned.1.call-done = (f32[128,2048]{1,0:T(8,128)}, f32[128,2048]{1,0:T(8,128)}) async-done(((f32[128,2048]{1,0:T(8,128)}, f32[128,2048]{1,0:T(8,128)}), (f32[128,2048]{1,0:T(8,128)}, f32[128,2048]{1,0:T(8,128)})) %all-reduce.25.cloned.1.call-update) | async-done | bytes 2097168 | tf_op jit(solution)/shard_map/psum | solution.py:26
  101.3 2.8 multiply_multiply_fusion
  104.1 5.5 all-to-all-start
  109.6 0.0 all-gather.2.cloned.1.call-start
  109.7 25.6 %all-to-all-done = f32[8,16,2048]{2,1,0:T(8,128)S(1)} async-done(((f32[8,16,2048]{2,1,0:T(8,128)}), f32[8,16,2048]{2,1,0:T(8,128)S(1)}, u32[]{:S(2)}, u32[]{:S(2)}) %all-to-all-start) | async-done | bytes 1048608 | tf_op jit(solution)/shard_map/all_to_all | solution.py:29
  135.3 0.1 copy.29
  135.3 0.7 constant_dynamic-slice_fusion
  136.1 0.6 all-reduce.13.cloned.1.call-start
  136.7 46.8 %all-gather.2.cloned.1.call-done = f32[128,4096]{1,0:T(8,128)} async-done(((f32[16,4096]{1,0:T(8,128)}), f32[128,4096]{1,0:T(8,128)}) %all-gather.2.cloned.1.call-update) | async-done | bytes 2097168 | tf_op jit(solution)/shard_map/all_gather | solution.py:31
  183.5 37.9 %select_add_fusion = f32[4096,2048]{1,0:T(8,128)} fusion(f32[4096,2048]{1,0:T(8,128)} %param.25, s32[2048]{0:T(1024)S(1)} %iota_add_fusion.1, s32[4096]{0:T(1024)S(1)} %iota_add_fusion, f32[128,4096]{1,0:T(8,128)} %all-gather.2.cloned.1.call-done, f32[128,2048]{1,0:T(8,128)} %multiply_multiply_fusion), kind=kOutput, calls=%fused_computation | convolution fusion | flops 12926844928 | bytes 70279168 | tf_op jit(solution)/shard_map/dot_general | solution.py:34
  221.5 0.8 slice.160
  222.3 0.1 copy.21
  222.4 0.9 fusion.38
  223.2 0.1 copy.22
  223.3 11.7 %cholesky.44 = f32[128,128]{1,0:T(8,128)S(1)} custom-call(f32[128,128]{1,0:T(8,128)S(1)} %copy.22), custom_call_target="Cholesky" | custom-call | tf_op jit(solution)/shard_map/jit(cholesky)/cholesky | solution.py:50
  235.1 0.6 compare_reduce_fusion.1
  235.7 1.2 select_select_fusion.3
  237.0 0.2 all-reduce.15.cloned.1.call-start
  237.2 30.0 %all-reduce.13.cloned.1.call-done = f32[128,128]{1,0:T(8,128)} async-done(((f32[128,128]{1,0:T(8,128)}), f32[128,128]{1,0:T(8,128)}) %all-reduce.13.cloned.1.call-update) | async-done | bytes 65552 | tf_op jit(solution)/shard_map/psum | solution.py:13
  267.2 0.8 select_bitcast_fusion.1
  268.0 9.8 %custom-call.10 = f32[1,128,128]{1,2,0:T(8,128)S(1)} custom-call(f32[1,128,128]{2,1,0:T(8,128)S(1)} %select_bitcast_fusion.1), custom_call_target="InvertDiagBlocksLowerTriangular" | custom-call | tf_op jit(solution)/shard_map/jit(_solve_triangular)/triangular_solve | solution.py:53
  277.8 6.8 fusion.5
  284.6 0.0 all-reduce.17.cloned.1.call-start
  284.7 0.7 compare_reduce_fusion.3
  285.4 101.7 %all-reduce.15.cloned.1.call-done = f32[4096,128]{1,0:T(8,128)} async-done(((f32[4096,128]{1,0:T(8,128)}), f32[4096,128]{1,0:T(8,128)}) %all-reduce.15.cloned.1.call-update) | async-done | bytes 2097168 | tf_op jit(solution)/shard_map/psum | solution.py:13
  387.1 2.4 dynamic-slice_select_fusion.1
  389.5 0.0 all-reduce.23.cloned.1.call-start
  389.6 9.8 %custom-call.12 = f32[1,128,128]{1,2,0:T(8,128)S(1)} custom-call(f32[1,128,128]{2,1,0:T(8,128)S(1)} %fusion.32), custom_call_target="InvertDiagBlocksLowerTriangular" | custom-call | tf_op jit(solution)/shard_map/jit(_solve_triangular)/triangular_solve | solution.py:70
  399.4 2.1 convolution_select_fusion.3
  401.5 24.0 %all-reduce.17.cloned.1.call-done = f32[2048,128]{1,0:T(8,128)} async-done(((f32[2048,128]{1,0:T(8,128)}), f32[2048,128]{1,0:T(8,128)}) %all-reduce.17.cloned.1.call-update) | async-done | bytes 1048592 | tf_op jit(solution)/shard_map/psum | solution.py:13
  425.5 34.3 %convolution_subtract_fusion.1 = f32[4096,2048]{1,0:T(8,128)} fusion(f32[4096,2048]{1,0:T(8,128)} %select_add_fusion, f32[4096,128]{1,0:T(8,128)S(1)} %copy-done, f32[2048,128]{1,0:T(8,128)} %all-reduce.17.cloned.1.call-done, pred[4096]{0:T(1024)(128)(4,1)S(1)} %get-tuple-element.85, pred[2048]{0:T(1024)(128)(4,1)S(1)} %fusion.47), kind=kOutput, calls=%fused_computation.2 | convolution fusion | flops 12894076928 | bytes 70260736 | tf_op jit(solution)/shard_map/dot_general | solution.py:63
  459.8 5.2 fusion.6
  465.0 0.8 slice.163
  465.9 0.1 copy.24
  466.0 0.9 fusion.36
  466.8 0.1 copy.25
  466.9 11.7 %cholesky.55 = f32[128,128]{1,0:T(8,128)S(1)} custom-call(f32[128,128]{1,0:T(8,128)S(1)} %copy.25), custom_call_target="Cholesky" | custom-call | tf_op jit(solution)/shard_map/jit(cholesky)/cholesky | solution.py:50
  478.7 0.7 compare_reduce_fusion
  479.3 1.3 select_select_fusion.2
  480.6 0.3 all-reduce.19.cloned.1.call-start
  480.9 33.0 %all-reduce.23.cloned.1.call-done = (f32[128,128]{1,0:T(8,128)}, f32[128,512]{1,0:T(8,128)}) async-done(((f32[128,128]{1,0:T(8,128)}, f32[128,512]{1,0:T(8,128)}), (f32[128,128]{1,0:T(8,128)}, f32[128,512]{1,0:T(8,128)})) %all-reduce.23.cloned.1.call-update) | async-done | bytes 327696 | tf_op jit(solution)/shard_map/psum | solution.py:13
  513.8 0.8 select_bitcast_fusion
  514.7 9.8 %custom-call.11 = f32[1,128,128]{1,2,0:T(8,128)S(1)} custom-call(f32[1,128,128]{2,1,0:T(8,128)S(1)} %select_bitcast_fusion), custom_call_target="InvertDiagBlocksLowerTriangular" | custom-call | tf_op jit(solution)/shard_map/jit(_solve_triangular)/triangular_solve | solution.py:53
  524.5 6.9 fusion.2
  531.4 0.0 all-reduce.21.cloned.1.call-start
  531.5 0.9 copy-done.4
  532.4 11.6 %convolution_subtract_fusion.3 = f32[4096,512]{1,0:T(8,128)} fusion(f32[4096,512]{1,0:T(8,128)} %param.26, f32[128,512]{1,0:T(8,128)S(1)} %copy-done.4, f32[4096,128]{1,0:T(8,128)S(1)} %copy-done, pred[4096]{0:T(1024)(128)(4,1)S(1)} %get-tuple-element.85), kind=kOutput, calls=%fused_computation.4 | convolution fusion | flops 3223846912 | bytes 19140608 | tf_op jit(solution)/shard_map/dot_general | solution.py:74
  544.0 1.7 fusion.29
  545.7 88.2 %all-reduce.19.cloned.1.call-done = f32[4096,128]{1,0:T(8,128)} async-done(((f32[4096,128]{1,0:T(8,128)}), f32[4096,128]{1,0:T(8,128)}) %all-reduce.19.cloned.1.call-update) | async-done | bytes 2097168 | tf_op jit(solution)/shard_map/psum | solution.py:13
  633.9 1.0 fusion.31
  634.9 9.8 %custom-call.13 = f32[1,128,128]{1,2,0:T(8,128)S(1)} custom-call(f32[1,128,128]{2,1,0:T(8,128)S(1)} %fusion.31), custom_call_target="InvertDiagBlocksLowerTriangular" | custom-call | tf_op jit(solution)/shard_map/jit(_solve_triangular)/triangular_solve | solution.py:70
  644.7 2.1 convolution_select_fusion.2
  646.8 2.3 dynamic-slice_select_fusion
  649.1 0.7 compare_reduce_fusion.2
  649.8 37.9 %all-reduce.21.cloned.1.call-done = (f32[2048,128]{1,0:T(8,128)}, f32[128,512]{1,0:T(8,128)}) async-done(((f32[2048,128]{1,0:T(8,128)}, f32[128,512]{1,0:T(8,128)}), (f32[2048,128]{1,0:T(8,128)}, f32[128,512]{1,0:T(8,128)})) %all-reduce.21.cloned.1.call-update) | async-done | bytes 1310736 | tf_op jit(solution)/shard_map/psum | solution.py:13
  687.7 9.8 %convolution_subtract_fusion.2 = f32[4096,512]{1,0:T(8,128)S(1)} fusion(f32[4096,512]{1,0:T(8,128)} %fusion.29, f32[128,512]{1,0:T(8,128)} %get-tuple-element.78, f32[4096,128]{1,0:T(8,128)S(1)} %copy-done.1, pred[4096]{0:T(1024)(128)(4,1)S(1)} %get-tuple-element.83), kind=kOutput, calls=%fused_computation.3 | convolution fusion | flops 3223846912 | bytes 19140608 | tf_op jit(solution)/shard_map/dot_general | solution.py:74
  697.4 0.1 fusion.27
  697.5 37.9 %convolution_subtract_fusion = f32[4096,2048]{1,0:T(8,128)} fusion(f32[4096,2048]{1,0:T(8,128)} %fusion.6, f32[4096,128]{1,0:T(8,128)S(1)} %copy-done.1, f32[2048,128]{1,0:T(8,128)S(1)} %copy-done.3, pred[4096]{0:T(1024)(128)(4,1)S(1)} %get-tuple-element.83, pred[2048]{0:T(1024)(128)(4,1)S(1)} %fusion.46), kind=kOutput, calls=%fused_computation.1 | convolution fusion | flops 12894076928 | bytes 70260736 | tf_op jit(solution)/shard_map/dot_general | solution.py:63
  735.4 5.2 fusion.7
  (33 shorter events, 0.3 us)
Async XLA Ops:
  7.2 94.2 %all-reduce.25.cloned.1.call-start = ((), (), s32[]{:S(2)}) async-start(), calls=%async_computation.8 | async-start | bytes 4194304 | tf_op jit(solution)/shard_map/psum | solution.py:26
  7.2 39.2 %slice-start = ((s8[8388608]{0:T(1024)(128)(4,1)}), s8[4194304]{0:T(1024)(128)(4,1)S(1)}, s32[]{:S(2)}) async-start(s8[8388608]{0:T(1024)(128)(4,1)} %bitcast.58), calls=%async_computation.9 | async-start | bytes 8388608
  40.6 5.8 slice-start.1
  104.1 31.1 %all-to-all-start = ((f32[8,16,2048]{2,1,0:T(8,128)}), f32[8,16,2048]{2,1,0:T(8,128)S(1)}, u32[]{:S(2)}, u32[]{:S(2)}) async-start(f32[8,16,2048]{2,1,0:T(8,128)} %bitcast), calls=%async_computation | async-start | bytes 2097152 | tf_op jit(solution)/shard_map/all_to_all | solution.py:29
  109.6 73.9 %all-gather.2.cloned.1.call-start = ((), (), s32[]{:S(2)}) async-start(), calls=%async_computation.1 | async-start | bytes 2359296 | tf_op jit(solution)/shard_map/all_gather | solution.py:31
  136.1 131.1 %all-reduce.13.cloned.1.call-start = ((), (), s32[]{:S(2)}) async-start(), calls=%async_computation.2 | async-start | bytes 131072 | tf_op jit(solution)/shard_map/psum | solution.py:13
  237.0 150.1 %all-reduce.15.cloned.1.call-start = ((), (), s32[]{:S(2)}) async-start(), calls=%async_computation.3 | async-start | bytes 4194304 | tf_op jit(solution)/shard_map/psum | solution.py:13
  284.6 140.9 %all-reduce.17.cloned.1.call-start = ((), (), s32[]{:S(2)}) async-start(), calls=%async_computation.4 | async-start | bytes 2097152 | tf_op jit(solution)/shard_map/psum | solution.py:13
  387.1 2.5 copy-start
  389.5 124.3 %all-reduce.23.cloned.1.call-start = ((), (), s32[]{:S(2)}) async-start(), calls=%async_computation.7 | async-start | bytes 655360 | tf_op jit(solution)/shard_map/psum | solution.py:13
  480.6 153.3 %all-reduce.19.cloned.1.call-start = ((), (), s32[]{:S(2)}) async-start(), calls=%async_computation.5 | async-start | bytes 4194304 | tf_op jit(solution)/shard_map/psum | solution.py:13
  531.4 0.9 copy-start.4
  531.4 156.2 %all-reduce.21.cloned.1.call-start = ((), (), s32[]{:S(2)}) async-start(), calls=%async_computation.6 | async-start | bytes 2621440 | tf_op jit(solution)/shard_map/psum | solution.py:13
  633.9 53.8 %copy-start.1 = (f32[4096,128]{1,0:T(8,128)S(1)}, f32[4096,128]{1,0:T(8,128)}, u32[]{:S(2)}) copy-start(f32[4096,128]{1,0:T(8,128)} %all-reduce.19.cloned.1.call-done) | copy-start | bytes 6291460
  687.7 9.8 %copy-start.5 = (f32[128,512]{1,0:T(8,128)S(1)}, f32[128,512]{1,0:T(8,128)}, u32[]{:S(2)}) copy-start(f32[128,512]{1,0:T(8,128)} %get-tuple-element.78) | copy-start | bytes 786436
  687.7 9.9 %copy-start.3 = (f32[2048,128]{1,0:T(8,128)S(1)}, f32[2048,128]{1,0:T(8,128)}, u32[]{:S(2)}) copy-start(f32[2048,128]{1,0:T(8,128)} %get-tuple-element.77) | copy-start | bytes 3145732
  697.5 37.9 %copy-start.2 = (f32[4096,512]{1,0:T(8,128)}, f32[4096,512]{1,0:T(8,128)S(1)}, u32[]{:S(2)}) copy-start(f32[4096,512]{1,0:T(8,128)S(1)} %fusion.27) | copy-start | bytes 25165828
Sparse Core Ops, SparseCore 0:
  48.8 52.4 all-reduce.24
  136.2 47.2 all-gather.1
  237.1 30.0 all-reduce.12
  284.8 102.2 all-reduce.14
  389.9 35.6 all-reduce.16
  480.7 33.0 all-reduce.22
  531.6 102.2 all-reduce.18
  649.2 38.3 all-reduce.20
where the time goes:
time: 752 us; the launch traced here: 748 us
  waiting for transfers between devices  440 us (59%)
  matrix products  157 us (21%)
  other arithmetic  91.9 us (12%)
  blocking collectives  33.4 us (4%)
  between operations  14.8 us (2%)
    psum x6, waiting for transfers between devices, from_root(): return lax.psum(kept, axis)  315 us
    dot_general x2, matrix products, local(): lax.dot_general(lower_rows, upper_cols, (((1,), (1,)), ((), ())), precisi...  72.1 us
    psum x1, waiting for transfers between devices, local(): gate, upward = lax.psum((gate_part, up_part), 'row')  52.7 us
    all_gather x1, waiting for transfers between devices, local(): row_keys = lax.all_gather(own_part, 'col', axis=0, tiled=True)  46.8 us
    dot_general x1, matrix products, local(): lax.dot_general(row_keys, keys, (((0,), (0,)), ((), ())), precision=lax.P...  37.9 us
    all_gather x1, blocking collectives, local(): tokens = lax.all_gather(hidden, 'col', axis=0, tiled=True)  33.4 us
    all_to_all x1, waiting for transfers between devices, local(): lax.all_to_all(keys, 'col', split_axis=0, concat_axis=1, tiled=True)  25.6 us
    another operation x6, other arithmetic, local(): pivot = jnp.linalg.cholesky(work[start:stop, start:stop])  24.8 us
  transfers between devices with their start and end apart: 9, of which 9 were waited for; matrix products, arithmetic and copies ran while one was open for 4% of the time, Pallas kernels for 0%

commit v1 on v0

--- a/solution.py
+++ b/solution.py
@@ -10,7 +10,7 @@
 
 def from_root(value, axis, source):
     kept = jnp.where(lax.axis_index(axis) == source, value, 0).astype(value.dtype)
-    return lax.psum(kept, axis)
+    return jnp.sum(lax.all_gather(kept, axis), axis=0)
 
 
 def local(hidden, w_gate, w_up, prior, rhs):

time: 752 us -> 957 us (1.27)
  waiting for transfers between devices: 440 us -> 618 us
  other arithmetic: 91.9 us -> 108 us
  blocking collectives: 33.4 us -> 45.5 us
    all_gather x0 -> x6, waiting for transfers between devices: none -> 493 us  [from_root(): return jnp.sum(lax.all_gather(kept, axis), axis=0)]
    psum x6 -> x0, waiting for transfers between devices: 315 us -> none  [from_root(): return lax.psum(kept, axis)]
    reduce_sum x0 -> x8, other arithmetic: none -> 21.4 us  [from_root(): return jnp.sum(lax.all_gather(kept, axis), axis=0)]
    all_gather x0 -> x2, blocking collectives: none -> 12.1 us  [from_root(): return jnp.sum(lax.all_gather(kept, axis), axis=0)]
  transfers between devices with their start and end apart: 9 -> 9, of which waited for: 9 -> 8; matrix products, arithmetic and copies ran while one was open for 4% -> 12% of each run, Pallas kernels for 0% -> 0%
where the time goes in v1:
time: 957 us; the launch traced here: 953 us
  waiting for transfers between devices  618 us (65%)
  matrix products  157 us (16%)
  other arithmetic  108 us (11%)
  blocking collectives  45.5 us (5%)
  between operations  14.6 us (2%)
    all_gather x6, waiting for transfers between devices, from_root(): return jnp.sum(lax.all_gather(kept, axis), axis=0)  493 us
    dot_general x2, matrix products, local(): lax.dot_general(lower_rows, upper_cols, (((1,), (1,)), ((), ())), precisi...  69.8 us
    psum x1, waiting for transfers between devices, local(): gate, upward = lax.psum((gate_part, up_part), 'row')  52.7 us
    all_gather x1, waiting for transfers between devices, local(): row_keys = lax.all_gather(own_part, 'col', axis=0, tiled=True)  46.8 us
    dot_general x1, matrix products, local(): lax.dot_general(row_keys, keys, (((0,), (0,)), ((), ())), precision=lax.P...  37.9 us
    all_gather x1, blocking collectives, local(): tokens = lax.all_gather(hidden, 'col', axis=0, tiled=True)  33.4 us
    all_to_all x1, waiting for transfers between devices, local(): lax.all_to_all(keys, 'col', split_axis=0, concat_axis=1, tiled=True)  25.6 us
    another operation x6, other arithmetic, local(): pivot = jnp.linalg.cholesky(work[start:stop, start:stop])  24.8 us
  transfers between devices with their start and end apart: 9, of which 8 were waited for; matrix products, arithmetic and copies ran while one was open for 12% of the time, Pallas kernels for 0%

profile of v1, /device:TPU:0, one launch (start us, length us, event | category | flops | bytes accessed | tf_op | source)
XLA Modules:
  0.0 953.3 jit_solution(9523099247252697107)
XLA Ops:
  7.2 33.4 %all_gather.54 = bf16[128,2048]{1,0:T(8,128)(2,1)S(1)} all-gather(bf16[16,2048]{1,0:T(8,128)(2,1)} %param.22), channel_id=1, replica_groups=mesh['row'=4,'col'=8] {'col'}, dimensions={0}, use_global_device_ids=true | all-gather | bytes 589824 | tf_op jit(solution)/shard_map/all_gather | solution.py:23
  40.6 5.8 fusion.53
  46.4 2.3 fusion.52
  48.7 52.7 %all-reduce.5.cloned.1.call-done = (f32[128,2048]{1,0:T(8,128)}, f32[128,2048]{1,0:T(8,128)}) async-done(((f32[128,2048]{1,0:T(8,128)}, f32[128,2048]{1,0:T(8,128)}), (f32[128,2048]{1,0:T(8,128)}, f32[128,2048]{1,0:T(8,128)})) %all-reduce.5.cloned.1.call-update) | async-done | bytes 2097168 | tf_op jit(solution)/shard_map/psum | solution.py:26
  101.3 2.8 multiply_multiply_fusion
  104.1 5.5 all-to-all-start
  109.7 25.6 %all-to-all-done = f32[8,16,2048]{2,1,0:T(8,128)S(1)} async-done(((f32[8,16,2048]{2,1,0:T(8,128)}), f32[8,16,2048]{2,1,0:T(8,128)S(1)}, u32[]{:S(2)}, u32[]{:S(2)}) %all-to-all-start) | async-done | bytes 1048608 | tf_op jit(solution)/shard_map/all_to_all | solution.py:29
  135.3 0.1 copy.29
  135.3 0.7 constant_dynamic-slice_fusion
  136.1 0.6 all-gather.18.cloned.1.call-start
  136.7 46.8 %all-gather.16.cloned.1.call-done = f32[128,4096]{1,0:T(8,128)} async-done(((f32[16,4096]{1,0:T(8,128)}), f32[128,4096]{1,0:T(8,128)}) %all-gather.16.cloned.1.call-update) | async-done | bytes 2097168 | tf_op jit(solution)/shard_map/all_gather | solution.py:31
  183.5 37.9 %select_add_fusion = f32[4096,2048]{1,0:T(8,128)} fusion(f32[4096,2048]{1,0:T(8,128)} %param.25, s32[2048]{0:T(1024)S(1)} %iota_add_fusion.1, s32[4096]{0:T(1024)S(1)} %iota_add_fusion, f32[128,4096]{1,0:T(8,128)} %all-gather.16.cloned.1.call-done, f32[128,2048]{1,0:T(8,128)} %multiply_multiply_fusion), kind=kOutput, calls=%fused_computation | convolution fusion | flops 12926844928 | bytes 70279168 | tf_op jit(solution)/shard_map/dot_general | solution.py:34
  221.5 0.8 slice.160
  222.3 0.1 copy.21
  222.4 0.9 fusion.38
  223.3 0.1 copy.22
  223.4 11.7 %cholesky.44 = f32[128,128]{1,0:T(8,128)S(1)} custom-call(f32[128,128]{1,0:T(8,128)S(1)} %copy.22), custom_call_target="Cholesky" | custom-call | tf_op jit(solution)/shard_map/jit(cholesky)/cholesky | solution.py:50
  235.1 0.6 compare_reduce_fusion.1
  235.7 0.7 select_select_fusion.3
  236.4 6.0 all-gather
  242.4 9.8 %custom-call.10 = f32[1,128,128]{1,2,0:T(8,128)S(1)} custom-call(f32[1,128,128]{2,1,0:T(8,128)S(1)} %select_bitcast_fusion.1), custom_call_target="InvertDiagBlocksLowerTriangular" | custom-call | tf_op jit(solution)/shard_map/jit(_solve_triangular)/triangular_solve | solution.py:53
  252.2 6.8 fusion.5
  259.0 0.0 all-gather.20.cloned.1.call-start
  259.1 225.9 %all-gather.18.cloned.1.call-done = f32[32768,128]{1,0:T(8,128)} async-done(((f32[4096,128]{1,0:T(8,128)}), f32[32768,128]{1,0:T(8,128)}) %all-gather.18.cloned.1.call-update) | async-done | bytes 16777232 | tf_op jit(solution)/shard_map/all_gather | solution.py:13
  485.0 6.8 reduce_sum.73
  491.8 1.0 dynamic-slice_select_fusion.1
  492.9 0.0 all-gather.26.cloned.1.call-start
  492.9 0.6 compare_reduce_fusion.3
  493.6 9.8 %custom-call.12 = f32[1,128,128]{1,2,0:T(8,128)S(1)} custom-call(f32[1,128,128]{2,1,0:T(8,128)S(1)} %fusion.32), custom_call_target="InvertDiagBlocksLowerTriangular" | custom-call | tf_op jit(solution)/shard_map/jit(_solve_triangular)/triangular_solve | solution.py:70
  503.4 2.1 convolution_select_fusion.3
  505.5 0.3 all-gather.22.cloned.1.call-start
  505.8 20.0 %all-gather.20.cloned.1.call-done = f32[8192,128]{1,0:T(8,128)} async-done(((f32[2048,128]{1,0:T(8,128)}), f32[8192,128]{1,0:T(8,128)}) %all-gather.20.cloned.1.call-update) | async-done | bytes 4194320 | tf_op jit(solution)/shard_map/all_gather | solution.py:13
  525.8 2.5 reduce_sum.74
  528.3 34.9 %convolution_subtract_fusion.1 = f32[4096,2048]{1,0:T(8,128)} fusion(f32[4096,2048]{1,0:T(8,128)} %select_add_fusion, f32[4096,128]{1,0:T(8,128)S(1)} %reduce_sum.73, f32[2048,128]{1,0:T(8,128)S(1)} %reduce_sum.74, pred[4096]{0:T(1024)(128)(4,1)S(1)} %get-tuple-element.81, pred[2048]{0:T(1024)(128)(4,1)S(1)} %fusion.47), kind=kOutput, calls=%fused_computation.2 | convolution fusion | flops 12894076928 | bytes 70260736 | tf_op jit(solution)/shard_map/dot_general | solution.py:63
  563.2 5.2 fusion.6
  568.3 0.8 slice.163
  569.2 0.1 copy.24
  569.3 0.9 fusion.36
  570.1 0.1 copy.25
  570.2 11.7 %cholesky.55 = f32[128,128]{1,0:T(8,128)S(1)} custom-call(f32[128,128]{1,0:T(8,128)S(1)} %copy.25), custom_call_target="Cholesky" | custom-call | tf_op jit(solution)/shard_map/jit(cholesky)/cholesky | solution.py:50
  582.0 0.6 compare_reduce_fusion
  582.6 0.7 select_select_fusion.2
  583.3 6.2 all-gather.3
  589.5 9.8 %custom-call.11 = f32[1,128,128]{1,2,0:T(8,128)S(1)} custom-call(f32[1,128,128]{2,1,0:T(8,128)S(1)} %select_bitcast_fusion), custom_call_target="InvertDiagBlocksLowerTriangular" | custom-call | tf_op jit(solution)/shard_map/jit(_solve_triangular)/triangular_solve | solution.py:53
  599.3 7.0 fusion.2
  606.3 0.0 all-gather.28.cloned.1.call-start
  606.4 1.3 reduce_sum.78
  607.7 11.9 %convolution_subtract_fusion.3 = f32[4096,512]{1,0:T(8,128)} fusion(f32[4096,512]{1,0:T(8,128)} %param.26, f32[128,512]{1,0:T(8,128)S(1)} %reduce_sum.78, f32[4096,128]{1,0:T(8,128)S(1)} %reduce_sum.73, pred[4096]{0:T(1024)(128)(4,1)S(1)} %get-tuple-element.81), kind=kOutput, calls=%fused_computation.4 | convolution fusion | flops 3223846912 | bytes 19140608 | tf_op jit(solution)/shard_map/dot_general | solution.py:74
  619.6 1.7 fusion.29
  621.3 212.5 %all-gather.22.cloned.1.call-done = f32[32768,128]{1,0:T(8,128)} async-done(((f32[4096,128]{1,0:T(8,128)}), f32[32768,128]{1,0:T(8,128)}) %all-gather.22.cloned.1.call-update) | async-done | bytes 16777232 | tf_op jit(solution)/shard_map/all_gather | solution.py:13
  833.9 6.8 reduce_sum.76
  840.7 9.8 %custom-call.13 = f32[1,128,128]{1,2,0:T(8,128)S(1)} custom-call(f32[1,128,128]{2,1,0:T(8,128)S(1)} %fusion.31), custom_call_target="InvertDiagBlocksLowerTriangular" | custom-call | tf_op jit(solution)/shard_map/jit(_solve_triangular)/triangular_solve | solution.py:70
  850.5 2.1 convolution_select_fusion.2
  852.6 0.2 all-gather.24.cloned.1.call-start
  852.8 1.1 dynamic-slice_select_fusion
  853.9 0.7 compare_reduce_fusion.2
  854.6 13.0 %all-gather.28.cloned.1.call-done = f32[512,512]{1,0:T(8,128)} async-done(((f32[128,512]{1,0:T(8,128)}), f32[512,512]{1,0:T(8,128)}) %all-gather.28.cloned.1.call-update) | async-done | bytes 1048592 | tf_op jit(solution)/shard_map/all_gather | solution.py:13
  867.6 1.3 reduce_sum.79
  869.0 11.8 %convolution_subtract_fusion.2 = f32[4096,512]{1,0:T(8,128)} fusion(f32[4096,512]{1,0:T(8,128)} %fusion.29, f32[128,512]{1,0:T(8,128)S(1)} %reduce_sum.79, f32[4096,128]{1,0:T(8,128)S(1)} %reduce_sum.76, pred[4096]{0:T(1024)(128)(4,1)S(1)} %get-tuple-element.79), kind=kOutput, calls=%fused_computation.3 | convolution fusion | flops 3223846912 | bytes 19140608 | tf_op jit(solution)/shard_map/dot_general | solution.py:74
  880.7 1.7 fusion.27
  882.4 21.2 %all-gather.24.cloned.1.call-done = f32[8192,128]{1,0:T(8,128)} async-done(((f32[2048,128]{1,0:T(8,128)}), f32[8192,128]{1,0:T(8,128)}) %all-gather.24.cloned.1.call-update) | async-done | bytes 4194320 | tf_op jit(solution)/shard_map/all_gather | solution.py:13
  903.7 2.5 reduce_sum.77
  906.2 34.9 %convolution_subtract_fusion = f32[4096,2048]{1,0:T(8,128)} fusion(f32[4096,2048]{1,0:T(8,128)} %fusion.6, f32[4096,128]{1,0:T(8,128)S(1)} %reduce_sum.76, f32[2048,128]{1,0:T(8,128)S(1)} %reduce_sum.77, pred[4096]{0:T(1024)(128)(4,1)S(1)} %get-tuple-element.79, pred[2048]{0:T(1024)(128)(4,1)S(1)} %fusion.46), kind=kOutput, calls=%fused_computation.1 | convolution fusion | flops 12894076928 | bytes 70260736 | tf_op jit(solution)/shard_map/dot_general | solution.py:63
  941.1 5.2 fusion.7
  (31 shorter events, 0.4 us)
Async XLA Ops:
  7.2 94.2 %all-reduce.5.cloned.1.call-start = ((), (), s32[]{:S(2)}) async-start(), calls=%async_computation.8 | async-start | bytes 4194304 | tf_op jit(solution)/shard_map/psum | solution.py:26
  7.2 39.2 %slice-start = ((s8[8388608]{0:T(1024)(128)(4,1)}), s8[4194304]{0:T(1024)(128)(4,1)S(1)}, s32[]{:S(2)}) async-start(s8[8388608]{0:T(1024)(128)(4,1)} %bitcast.66), calls=%async_computation.9 | async-start | bytes 8388608
  40.6 5.8 slice-start.1
  104.1 31.1 %all-to-all-start = ((f32[8,16,2048]{2,1,0:T(8,128)}), f32[8,16,2048]{2,1,0:T(8,128)S(1)}, u32[]{:S(2)}, u32[]{:S(2)}) async-start(f32[8,16,2048]{2,1,0:T(8,128)} %bitcast), calls=%async_computation | async-start | bytes 2097152 | tf_op jit(solution)/shard_map/all_to_all | solution.py:29
  109.6 73.9 %all-gather.16.cloned.1.call-start = ((), (), s32[]{:S(2)}) async-start(), calls=%async_computation.1 | async-start | bytes 2359296 | tf_op jit(solution)/shard_map/all_gather | solution.py:31
  136.1 348.9 %all-gather.18.cloned.1.call-start = ((), (), s32[]{:S(2)}) async-start(), calls=%async_computation.2 | async-start | bytes 18874368 | tf_op jit(solution)/shard_map/all_gather | solution.py:13
  259.0 266.8 %all-gather.20.cloned.1.call-start = ((), (), s32[]{:S(2)}) async-start(), calls=%async_computation.3 | async-start | bytes 5242880 | tf_op jit(solution)/shard_map/all_gather | solution.py:13
  492.9 113.5 %all-gather.26.cloned.1.call-start = ((), (), s32[]{:S(2)}) async-start(), calls=%async_computation.6 | async-start | bytes 1310720 | tf_op jit(solution)/shard_map/all_gather | solution.py:13
  505.5 328.3 %all-gather.22.cloned.1.call-start = ((), (), s32[]{:S(2)}) async-start(), calls=%async_computation.4 | async-start | bytes 18874368 | tf_op jit(solution)/shard_map/all_gather | solution.py:13
  606.3 261.3 %all-gather.28.cloned.1.call-start = ((), (), s32[]{:S(2)}) async-start(), calls=%async_computation.7 | async-start | bytes 1310720 | tf_op jit(solution)/shard_map/all_gather | solution.py:13
  852.6 51.1 %all-gather.24.cloned.1.call-start = ((), (), s32[]{:S(2)}) async-start(), calls=%async_computation.5 | async-start | bytes 5242880 | tf_op jit(solution)/shard_map/all_gather | solution.py:13
Sparse Core Ops, SparseCore 0:
  48.8 52.4 all-reduce.4
  136.2 47.2 all-gather.15
  259.1 225.7 all-gather.17
  493.0 32.7 all-gather.19
  527.2 16.7 all-gather.25
  606.4 227.3 all-gather.21
  852.7 14.8 all-gather.27
  869.2 34.4 all-gather.23
